TPU v7x, 256 devices: a whole 4x4x8 slice. The times are simulated.
256 devices in a mesh: rows: 32 (over z, y), samp: 8 (over x, core).
Axes of the slice: x: 4, y: 4, z: 8, core: 2. Of those that a mesh axis runs over, the one named last changes fastest.
Arguments:
- coupling_tiles: bfloat16 [512, 32, 128, 128], P('rows', 'samp'), may hold values from -0.09375 to 0.09375
- tile_columns: int32 [512, 32], P('rows', 'samp'), may hold values from 0 to 511, as said below
- sample_matrix: bfloat16 [65536, 512], P('rows'), may hold values from -6 to 6
- phi_leaf: float32 [512, 256], replicated, may hold values from -0.25 to 0.25
- phi_pair: float32 [512, 256], replicated, may hold values from -0.25 to 0.25
- phi_quad: float32 [512, 256], replicated, may hold values from -0.25 to 0.25
Outputs:
- leaf_basis: float32 [65536, 256], P('rows')
- nested_transfer: float32 [8192, 256], P('rows')
- sample_approx: float32 [65536, 512], P('rows', 'samp')
Inputs may be any that keep to these rules, and one draw needn't show every extreme that they name: `tile_columns`: the 32 tile columns of a tile row are distinct and lie in the leaf block of that row or in one of the two leaf blocks beside it (16 tile rows to a leaf block).
All inputs are finite; a program needn't handle non-finite values.
Results may differ from a plain program's by a relative error of at most 0.0003.
Values may be sent and summed in bfloat16 or wider, within the bound.
A program may use at most 128 MiB of HBM per device.

v0:
```python
import jax
import jax.numpy as jnp
from jax import lax
from jax.sharding import PartitionSpec as P

NS_ITERS = 5
HIGH = lax.Precision.HIGHEST


def with_halo(block, sides, width):
    for axis, dim in sides:
        count = lax.axis_size(axis)
        forward = [(i, i + 1) for i in range(count - 1)]
        backward = [(target, source) for source, target in forward]
        low = lax.ppermute(
            lax.slice_in_dim(block, block.shape[dim] - width, None, axis=dim), axis, forward
        )
        high = lax.ppermute(lax.slice_in_dim(block, 0, width, axis=dim), axis, backward)
        block = jnp.concatenate([low, block, high], axis=dim)
    return block


def swapped(value, axis, distance):
    return lax.ppermute(value, axis, [(i, i ^ 1 << distance) for i in range(lax.axis_size(axis))])


def product(left, right):
    return jnp.dot(left, right, precision=HIGH, preferred_element_type=jnp.float32)


def orthogonal(matrix):
    gram_matrix = product(matrix.T, matrix)
    norm_scale = jnp.sqrt(jnp.sum(gram_matrix * gram_matrix)) + 1e-06
    identity = jnp.eye(gram_matrix.shape[0], dtype=jnp.float32)
    iterate = gram_matrix / norm_scale
    inverse_root = identity
    for step in range(NS_ITERS):
        factor = 1.5 * identity - 0.5 * product(inverse_root, iterate)
        iterate = product(iterate, factor)
        inverse_root = product(factor, inverse_root)
    return product(matrix, inverse_root) / jnp.sqrt(norm_scale)


def stack_pair(mine, other, which_bit):
    lower = jnp.where(which_bit == 0, mine, other)
    higher = jnp.where(which_bit == 0, other, mine)
    return jnp.concatenate([lower, higher], axis=0)


def on_device(coupling_tiles, tile_columns, sample_matrix, phi_leaf, phi_pair, phi_quad):
    per_leaf = 16
    leaf_rows = sample_matrix.shape[0]
    sample_cols = sample_matrix.shape[1]
    row_index = lax.axis_index("rows")
    extended = with_halo(sample_matrix, (("rows", 0),), leaf_rows)
    blocks = extended.reshape(3 * per_leaf, leaf_rows // per_leaf, sample_cols)
    local_columns = tile_columns - (row_index - 1) * per_leaf
    picked = jnp.take(blocks, local_columns, axis=0)
    partial_value = jnp.einsum(
        "tkab,tkbs->tas", coupling_tiles, picked, preferred_element_type=jnp.float32
    )
    partial_value = partial_value.reshape(leaf_rows, sample_cols)
    samp_count = lax.axis_size("samp")
    samp_index = lax.axis_index("samp")
    share_cols = sample_cols // samp_count
    sample = lax.psum(partial_value, "samp")

    def sketch(stacked, phi_matrix):
        return product(stacked, phi_matrix)

    def merge_level(stacked, phi_matrix):
        basis_now = orthogonal(sketch(stacked, phi_matrix))
        return (basis_now, product(basis_now.T, stacked))

    basis, coarse = merge_level(sample, phi_leaf)
    sibling_bit = row_index % 2
    cousin_bit = row_index // 2 % 2
    pair = stack_pair(coarse, swapped(coarse, "rows", 0), sibling_bit)
    upper, middle = merge_level(pair, phi_pair)
    quad = stack_pair(middle, swapped(middle, "rows", 1), cousin_bit)
    top, summary = merge_level(quad, phi_quad)
    rank_leaf = coarse.shape[0]
    rank_pair = middle.shape[0]
    own_upper = lax.dynamic_slice_in_dim(upper, sibling_bit * rank_leaf, rank_leaf, 0)
    own_top = lax.dynamic_slice_in_dim(top, cousin_bit * rank_pair, rank_pair, 0)
    nested = product(own_upper, own_top)
    approx = product(
        basis,
        product(nested, lax.dynamic_slice_in_dim(summary, samp_index * share_cols, share_cols, 1)),
    )
    return (basis, nested, approx)


def solution(mesh):
    return jax.shard_map(
        on_device,
        mesh=mesh,
        in_specs=(P("rows", "samp", None, None), P("rows", "samp"), P("rows", None), P(), P(), P()),
        out_specs=(P("rows", None), P("rows", None), P("rows", "samp")),
        check_vma=False,
    )
```

profile of v0, /device:TPU:7, one launch (start us, length us, event | category | flops | bytes accessed | tf_op | source)
XLA Modules:
  0.0 261.3 jit_solution(8823519993755245035)
XLA Ops:
  7.2 4.7 %collective-permute-start = (bf16[2048,512]{1,0:T(8,128)(2,1)}, bf16[2048,512]{1,0:T(8,128)(2,1)}, u32[]{:S(2)}, u32[]{:S(2)}) collective-permute-start(bf16[2048,512]{1,0:T(8,128)(2,1)} %param.8), channel_id=1, source_target_pairs={{0,8},{8,16},{16,24},{24,32},{32,40},{40,48},{48,56},{56,64},{64,7... | collective-permute-start | bytes 6291464 | tf_op jit(solution)/shard_map/ppermute | solution.py:15
  11.9 1.3 collective-permute-start.1
  13.2 0.7 compare_and_fusion
  14.1 41.0 %collective-permute-done = bf16[2048,512]{1,0:T(8,128)(2,1)} collective-permute-done((bf16[2048,512]{1,0:T(8,128)(2,1)}, bf16[2048,512]{1,0:T(8,128)(2,1)}, u32[]{:S(2)}, u32[]{:S(2)}) %collective-permute-start) | collective-permute-done | bytes 2097184 | tf_op jit(solution)/shard_map/ppermute | solution.py:15
  55.2 5.1 %collective-permute-done.1 = bf16[2048,512]{1,0:T(8,128)(2,1)} collective-permute-done((bf16[2048,512]{1,0:T(8,128)(2,1)}, bf16[2048,512]{1,0:T(8,128)(2,1)}, u32[]{:S(2)}, u32[]{:S(2)}) %collective-permute-start.1) | collective-permute-done | bytes 2097184 | tf_op jit(solution)/shard_map/ppermute | solution.py:18
  60.3 6.0 %pad_maximum_fusion = bf16[6144,512]{1,0:T(8,128)(2,1)} fusion(bf16[2048,512]{1,0:T(8,128)(2,1)} %collective-permute-done.1, bf16[2048,512]{1,0:T(8,128)(2,1)} %param.8, bf16[2048,512]{1,0:T(8,128)(2,1)} %collective-permute-done), kind=kLoop, calls=%fused_computation.4 | loop fusion | flops 18874368 | bytes 12582912 | tf_op jit(solution)/shard_map/concatenate | solution.py:19
  66.2 8.3 %gather_fusion = bf16[64,128,512]{2,1,0:T(8,128)(2,1)} fusion(bf16[48,128,512]{2,1,0:T(8,128)(2,1)} %bitcast.104, s32[1024]{0:T(1024)S(1)} %pad_clamp_fusion), kind=kCustom, calls=%fused_computation | custom fusion | bytes 16777472 | tf_op jit(solution)/shard_map/jit(_take)/gather | solution.py:58
  74.6 7.1 %fusion = f32[16,512,128,1]{1,2,3,0:T(8,128)} fusion(bf16[16,4,128,128]{3,2,1,0:T(8,128)(2,1)S(1)} %copy-done, bf16[16,4,128,512]{3,2,1,0:T(8,128)(2,1)} %bitcast.105, pred[16,4]{1,0:T(8,128)(4,1)S(1)} %copy.11), kind=kOutput, calls=%fused_computation.1 | convolution fusion | flops 1077936128 | bytes 14680128 | tf_op jit(solution)/shard_map/tkab,tkbs->tas/dot_general | solution.py:59
  81.7 81.9 %all-reduce.2.cloned.1.call-done = f32[2048,512]{1,0:T(8,128)} async-done(((f32[2048,512]{1,0:T(8,128)}), f32[2048,512]{1,0:T(8,128)}) %all-reduce.2.cloned.1.call-update) | async-done | bytes 4194320 | tf_op jit(solution)/shard_map/psum | solution.py:66
  163.6 5.7 %fusion.26 = f32[2048,256]{1,0:T(8,128)S(1)} fusion(f32[2048,512]{1,0:T(8,128)} %all-reduce.2.cloned.1.call-done, f32[512,256]{1,0:T(8,128)S(1)} %copy-done.11), kind=kOutput, calls=%fused_computation.77 | convolution fusion | flops 3221225472 | bytes 6815744 | tf_op jit(solution)/shard_map/dot_general | solution.py:28
  169.3 1.3 copy-done.1
  170.7 4.2 %multiply_reduce_fusion.2 = (f32[]{:T(128)}, f32[256,256]{1,0:T(8,128)S(1)}) fusion(f32[2048,256]{1,0:T(8,128)S(1)} %fusion.26), kind=kOutput, calls=%fused_computation.50 | convolution fusion | flops 1610743808 | bytes 2359300 | tf_op jit(solution)/shard_map/dot_general | solution.py:28
  175.9 0.4 fusion.16
  176.5 0.4 select_subtract_fusion.13
  178.9 0.4 select_subtract_fusion.11
  180.1 0.4 select_subtract_fusion.10
  180.9 3.7 %convolution_divide_fusion = f32[2048,256]{1,0:T(8,128)S(1)} fusion(f32[2048,256]{1,0:T(8,128)} %copy-done.1, f32[256,256]{1,0:T(8,128)S(1)} %fusion.33, f32[]{:T(128)S(6)} %sqrt.19), kind=kOutput, calls=%fused_computation.6 | convolution fusion | flops 1611137024 | bytes 4456452 | tf_op jit(solution)/shard_map/dot_general | solution.py:28
  184.6 4.0 %fusion.34 = f32[256,512]{1,0:T(8,128)S(1)} fusion(f32[2048,256]{1,0:T(8,128)S(1)} %convolution_divide_fusion, f32[2048,512]{1,0:T(8,128)S(1)} %copy-done.2), kind=kOutput, calls=%fused_computation.85 | convolution fusion | flops 3221225472 | bytes 6815744 | tf_op jit(solution)/shard_map/dot_general | solution.py:28
  188.6 1.3 collective-permute-start.2
  189.9 11.4 %collective-permute-done.2 = f32[256,512]{1,0:T(8,128)} collective-permute-done((f32[256,512]{1,0:T(8,128)S(1)}, f32[256,512]{1,0:T(8,128)}, u32[]{:S(2)}, u32[]{:S(2)}) %collective-permute-start.2) | collective-permute-done | bytes 524320 | tf_op jit(solution)/shard_map/ppermute | solution.py:24
  201.3 1.3 broadcast_select_fusion.3
  202.6 2.0 fusion.7
  204.7 0.8 copy-done.6
  205.4 1.6 multiply_reduce_fusion.1
  208.1 0.4 fusion.17
  208.8 0.4 select_subtract_fusion.8
  209.9 0.4 select_subtract_fusion.7
  211.5 1.1 fusion.40
  213.0 1.3 select_subtract_fusion.5
  214.7 1.6 convolution_divide_fusion.2
  216.4 1.9 fusion.6
  218.2 2.9 %collective-permute-start.3 = (f32[256,512]{1,0:T(8,128)}, f32[256,512]{1,0:T(8,128)}, u32[]{:S(2)}, u32[]{:S(2)}) collective-permute-start(f32[256,512]{1,0:T(8,128)} %fusion.6), channel_id=1, source_target_pairs={{0,16},{8,24},{16,0},{24,8},{32,48},{40,56},{48,32},{56,40},{64,80... | collective-permute-start | bytes 1572872 | tf_op jit(solution)/shard_map/ppermute | solution.py:24
  221.1 12.9 %collective-permute-done.3 = f32[256,512]{1,0:T(8,128)} collective-permute-done((f32[256,512]{1,0:T(8,128)}, f32[256,512]{1,0:T(8,128)}, u32[]{:S(2)}, u32[]{:S(2)}) %collective-permute-start.3) | collective-permute-done | bytes 524320 | tf_op jit(solution)/shard_map/ppermute | solution.py:24
  234.1 1.3 broadcast_select_fusion.1
  235.4 2.0 fusion.5
  237.4 0.8 copy-done.5
  238.2 1.6 multiply_reduce_fusion
  240.8 0.4 fusion.18
  241.5 0.4 select_subtract_fusion.3
  242.7 0.4 select_subtract_fusion.2
  243.8 0.4 select_subtract_fusion.1
  244.2 1.1 fusion.47
  245.8 1.5 select_subtract_fusion
  247.7 1.6 convolution_divide_fusion.1
  249.3 1.1 fusion.4
  250.4 0.4 fusion.8
  250.8 0.5 fusion.14
  251.2 3.0 %fusion.49 = f32[2048,64]{0,1:T(8,128)} fusion(f32[2048,256]{1,0:T(8,128)S(1)} %copy-done.4, f32[256,64]{1,0:T(8,128)S(1)} %fusion.14), kind=kOutput, calls=%fused_computation.100 | convolution fusion | flops 402653184 | bytes 2686976 | tf_op jit(solution)/shard_map/dot_general | solution.py:28
  (54 shorter events, 10.1 us)
Async XLA Ops:
  7.2 67.4 %copy-start = (bf16[16,4,128,128]{3,2,1,0:T(8,128)(2,1)S(1)}, bf16[16,4,128,128]{3,2,1,0:T(8,128)(2,1)}, u32[]{:S(2)}) copy-start(bf16[16,4,128,128]{3,2,1,0:T(8,128)(2,1)} %param.6) | copy-start | bytes 6291460
  7.2 156.4 %all-reduce.2.cloned.1.call-start = ((), (), s32[]{:S(2)}) async-start(), calls=%async_computation | async-start | bytes 8388608 | tf_op jit(solution)/shard_map/psum | solution.py:66
  7.2 47.9 %collective-permute-start = (bf16[2048,512]{1,0:T(8,128)(2,1)}, bf16[2048,512]{1,0:T(8,128)(2,1)}, u32[]{:S(2)}, u32[]{:S(2)}) collective-permute-start(bf16[2048,512]{1,0:T(8,128)(2,1)} %param.8), channel_id=1, source_target_pairs={{0,8},{8,16},{16,24},{24,32},{32,40},{40,48},{48,56},{56,64},{64,7... | collective-permute-start | bytes 6291464 | tf_op jit(solution)/shard_map/ppermute | solution.py:15
  11.9 48.4 %collective-permute-start.1 = (bf16[2048,512]{1,0:T(8,128)(2,1)}, bf16[2048,512]{1,0:T(8,128)(2,1)}, u32[]{:S(2)}, u32[]{:S(2)}) collective-permute-start(bf16[2048,512]{1,0:T(8,128)(2,1)} %param.8), channel_id=1, source_target_pairs={{8,0},{16,8},{24,16},{32,24},{40,32},{48,40},{56,48},{64,56},{72,6... | collective-permute-start | bytes 6291464 | tf_op jit(solution)/shard_map/ppermute | solution.py:18
  81.7 82.0 %copy-start.11 = (f32[512,256]{1,0:T(8,128)S(1)}, f32[512,256]{1,0:T(8,128)}, u32[]{:S(2)}) copy-start(f32[512,256]{1,0:T(8,128)} %param.9) | copy-start | bytes 1572868
  169.3 1.3 copy-start.1
  180.5 4.1 %copy-start.2 = (f32[2048,512]{1,0:T(8,128)S(1)}, f32[2048,512]{1,0:T(8,128)}, u32[]{:S(2)}) copy-start(f32[2048,512]{1,0:T(8,128)} %all-reduce.2.cloned.1.call-done) | copy-start | bytes 12582916
  184.6 4.0 %copy-start.3 = (f32[2048,256]{1,0:T(8,128)}, f32[2048,256]{1,0:T(8,128)S(1)}, u32[]{:S(2)}) copy-start(f32[2048,256]{1,0:T(8,128)S(1)} %convolution_divide_fusion) | copy-start | bytes 6291460
  188.6 1.3 copy-start.7
  188.6 12.7 %collective-permute-start.2 = (f32[256,512]{1,0:T(8,128)S(1)}, f32[256,512]{1,0:T(8,128)}, u32[]{:S(2)}, u32[]{:S(2)}) collective-permute-start(f32[256,512]{1,0:T(8,128)S(1)} %fusion.34), channel_id=1, source_target_pairs={{0,8},{8,0},{16,24},{24,16},{32,40},{40,32},{48,56},{56,48},{64,72... | collective-permute-start | bytes 1572872 | tf_op jit(solution)/shard_map/ppermute | solution.py:24
  204.6 0.8 copy-start.6
  216.3 1.9 copy-start.8
  218.2 15.9 %collective-permute-start.3 = (f32[256,512]{1,0:T(8,128)}, f32[256,512]{1,0:T(8,128)}, u32[]{:S(2)}, u32[]{:S(2)}) collective-permute-start(f32[256,512]{1,0:T(8,128)} %fusion.6), channel_id=1, source_target_pairs={{0,16},{8,24},{16,0},{24,8},{32,48},{40,56},{48,32},{56,40},{64,80... | collective-permute-start | bytes 1572872 | tf_op jit(solution)/shard_map/ppermute | solution.py:24
  237.4 0.8 copy-start.5
  245.8 4.6 %copy-start.9 = (f32[512,256]{1,0:T(8,128)S(1)}, f32[512,256]{1,0:T(8,128)}, u32[]{:S(2)}) copy-start(f32[512,256]{1,0:T(8,128)} %copy-done.8) | copy-start | bytes 1572868
  245.8 5.5 %copy-start.4 = (f32[2048,256]{1,0:T(8,128)S(1)}, f32[2048,256]{1,0:T(8,128)}, u32[]{:S(2)}) copy-start(f32[2048,256]{1,0:T(8,128)} %copy-done.3) | copy-start | bytes 6291460
  250.8 3.5 %copy-start.10 = (f32[256,256]{1,0:T(8,128)}, f32[256,256]{1,0:T(8,128)S(1)}, u32[]{:S(2)}) copy-start(f32[256,256]{1,0:T(8,128)S(1)} %fusion.8) | copy-start | bytes 786436
Sparse Core Ops, SparseCore 0:
  81.8 81.7 all-reduce.1
where the time goes:
time: 266 us; the launch traced here: 261 us
  waiting for transfers between devices  152 us (57%)
  matrix products  60.9 us (23%)
  between operations  17 us (6%)
  local copies, waits for them, and re-layouts  11.5 us (4%)
  starting transfers between devices  10.2 us (4%)
  other arithmetic  9.28 us (3%)
    psum x1, waiting for transfers between devices, on_device(): sample = lax.psum(partial_value, 'samp')  81.9 us
    dot_general x57, matrix products, product(): jnp.dot(left, right, precision=HIGH, preferred_element_type=jnp.float32)  53.8 us
    ppermute x1, waiting for transfers between devices, with_halo(): lax.ppermute(lax.slice_in_dim(block, block.shape[dim] - width, None, axis...  41 us
    ppermute x2, waiting for transfers between devices, swapped(): lax.ppermute(value, axis, [(i, i ^ 1 << distance) for i in range(lax.axis...  24.3 us
    gather x1, local copies, waits for them, and re-layouts, on_device(): picked = jnp.take(blocks, local_columns, axis=0)  8.31 us
    dot_general x1, matrix products, on_device(): jnp.einsum('tkab,tkbs->tas', coupling_tiles, picked, preferred_element_ty...  7.1 us
    concatenate x1, other arithmetic, with_halo(): block = jnp.concatenate([low, block, high], axis=dim)  5.99 us
  transfers between devices with their start and end apart: 5, of which 5 were waited for; matrix products, arithmetic and copies ran while one was open for 0% of the time, Pallas kernels for 0%

commit v1 on v0

--- a/solution.py
+++ b/solution.py
@@ -63,7 +63,8 @@
     samp_count = lax.axis_size("samp")
     samp_index = lax.axis_index("samp")
     share_cols = sample_cols // samp_count
-    sample = lax.psum(partial_value, "samp")
+    parts = lax.all_gather(partial_value, "samp", axis=0, tiled=False)
+    sample = parts.sum(axis=0)
 
     def sketch(stacked, phi_matrix):
         return product(stacked, phi_matrix)

time: 266 us -> 355 us (1.33)
  the two profiles are of different devices: /device:TPU:7 before, /device:TPU:2 now
where the time goes in v1:
time: 355 us; the launch traced here: 350 us
  waiting for transfers between devices  233 us (66%)
  matrix products  57.7 us (16%)
  other arithmetic  22 us (6%)
  between operations  17 us (5%)
  starting transfers between devices  11.1 us (3%)
  local copies, waits for them, and re-layouts  8.64 us (2%)
    all_gather x1, waiting for transfers between devices, on_device(): parts = lax.all_gather(partial_value, 'samp', axis=0, tiled=False)  162 us
    dot_general x57, matrix products, product(): jnp.dot(left, right, precision=HIGH, preferred_element_type=jnp.float32)  50.5 us
    ppermute x1, waiting for transfers between devices, with_halo(): lax.ppermute(lax.slice_in_dim(block, block.shape[dim] - width, None, axis...  41.6 us
    ppermute x2, waiting for transfers between devices, swapped(): lax.ppermute(value, axis, [(i, i ^ 1 << distance) for i in range(lax.axis...  24.4 us
    reduce_sum x1, other arithmetic, on_device(): sample = parts.sum(axis=0)  15.1 us
    gather x1, local copies, waits for them, and re-layouts, on_device(): picked = jnp.take(blocks, local_columns, axis=0)  8.32 us
    dot_general x1, matrix products, on_device(): jnp.einsum('tkab,tkbs->tas', coupling_tiles, picked, preferred_element_ty...  7.19 us
  transfers between devices with their start and end apart: 5, of which 5 were waited for; matrix products, arithmetic and copies ran while one was open for 0% of the time, Pallas kernels for 0%

profile of v1, /device:TPU:2, one launch (start us, length us, event | category | flops | bytes accessed | tf_op | source)
XLA Modules:
  0.0 350.0 jit_solution(13682694166665754532)
XLA Ops:
  7.2 4.9 %collective-permute-start = (bf16[2048,512]{1,0:T(8,128)(2,1)}, bf16[2048,512]{1,0:T(8,128)(2,1)}, u32[]{:S(2)}, u32[]{:S(2)}) collective-permute-start(bf16[2048,512]{1,0:T(8,128)(2,1)} %param.8), channel_id=1, source_target_pairs={{0,8},{8,16},{16,24},{24,32},{32,40},{40,48},{48,56},{56,64},{64,7... | collective-permute-start | bytes 6291464 | tf_op jit(solution)/shard_map/ppermute | solution.py:15
  12.2 1.3 collective-permute-start.1
  13.5 0.7 compare_and_fusion
  14.4 41.6 %collective-permute-done = bf16[2048,512]{1,0:T(8,128)(2,1)} collective-permute-done((bf16[2048,512]{1,0:T(8,128)(2,1)}, bf16[2048,512]{1,0:T(8,128)(2,1)}, u32[]{:S(2)}, u32[]{:S(2)}) %collective-permute-start) | collective-permute-done | bytes 2097184 | tf_op jit(solution)/shard_map/ppermute | solution.py:15
  56.0 5.4 %collective-permute-done.1 = bf16[2048,512]{1,0:T(8,128)(2,1)} collective-permute-done((bf16[2048,512]{1,0:T(8,128)(2,1)}, bf16[2048,512]{1,0:T(8,128)(2,1)}, u32[]{:S(2)}, u32[]{:S(2)}) %collective-permute-start.1) | collective-permute-done | bytes 2097184 | tf_op jit(solution)/shard_map/ppermute | solution.py:18
  61.5 6.0 %pad_maximum_fusion = bf16[6144,512]{1,0:T(8,128)(2,1)} fusion(bf16[2048,512]{1,0:T(8,128)(2,1)} %collective-permute-done.1, bf16[2048,512]{1,0:T(8,128)(2,1)} %param.8, bf16[2048,512]{1,0:T(8,128)(2,1)} %collective-permute-done), kind=kLoop, calls=%fused_computation.4 | loop fusion | flops 18874368 | bytes 12582912 | tf_op jit(solution)/shard_map/concatenate | solution.py:19
  67.5 8.3 %gather_fusion = bf16[64,128,512]{2,1,0:T(8,128)(2,1)} fusion(bf16[48,128,512]{2,1,0:T(8,128)(2,1)} %bitcast.104, s32[1024]{0:T(1024)S(1)} %pad_clamp_fusion), kind=kCustom, calls=%fused_computation | custom fusion | bytes 16777472 | tf_op jit(solution)/shard_map/jit(_take)/gather | solution.py:58
  75.8 7.2 %fusion = f32[16,512,128,1]{1,2,3,0:T(8,128)} fusion(bf16[16,4,128,128]{3,2,1,0:T(8,128)(2,1)S(1)} %copy-done, bf16[16,4,128,512]{3,2,1,0:T(8,128)(2,1)} %bitcast.105, pred[16,4]{1,0:T(8,128)(4,1)S(1)} %copy.13), kind=kOutput, calls=%fused_computation.1 | convolution fusion | flops 1077936128 | bytes 14680128 | tf_op jit(solution)/shard_map/tkab,tkbs->tas/dot_general | solution.py:59
  83.0 162.0 %all-gather.2.cloned.1.call-done = f32[8,2048,512]{2,1,0:T(8,128)} async-done(((f32[1,2048,512]{2,1,0:T(8,128)}), f32[8,2048,512]{2,1,0:T(8,128)}) %all-gather.2.cloned.1.call-update) | async-done | bytes 33554448 | tf_op jit(solution)/shard_map/all_gather | solution.py:66
  245.0 15.1 %reduce_sum.36 = f32[2048,512]{1,0:T(8,128)} reduce(f32[8,2048,512]{2,1,0:T(8,128)} %all-gather.2.cloned.1.call-done, f32[]{:T(128)} %constant.62.clone.1), dimensions={0}, to_apply=%region_0.1 | reduce | flops 7340032 | bytes 37748740 | tf_op jit(solution)/shard_map/reduce_sum | solution.py:67
  260.2 5.7 %fusion.26 = f32[2048,256]{1,0:T(8,128)S(1)} fusion(f32[2048,512]{1,0:T(8,128)} %reduce_sum.36, f32[512,256]{1,0:T(8,128)S(1)} %copy-done.8), kind=kOutput, calls=%fused_computation.77 | convolution fusion | flops 3221225472 | bytes 6815744 | tf_op jit(solution)/shard_map/dot_general | solution.py:28
  265.8 4.1 %multiply_reduce_fusion.2 = (f32[]{:T(128)}, f32[256,256]{1,0:T(8,128)S(1)}) fusion(f32[2048,256]{1,0:T(8,128)S(1)} %fusion.26), kind=kOutput, calls=%fused_computation.50 | convolution fusion | flops 1610743808 | bytes 2359300 | tf_op jit(solution)/shard_map/dot_general | solution.py:28
  270.9 0.4 fusion.14
  271.6 0.4 select_subtract_fusion.13
  272.8 0.4 select_subtract_fusion.12
  273.9 0.4 select_subtract_fusion.11
  274.3 0.4 fusion.32
  274.7 0.4 fusion.31
  275.2 0.4 select_subtract_fusion.10
  275.6 0.4 fusion.33
  275.9 1.9 convolution_divide_fusion
  277.9 4.0 %fusion.34 = f32[256,512]{1,0:T(8,128)S(1)} fusion(f32[2048,256]{1,0:T(8,128)S(1)} %convolution_divide_fusion, f32[2048,512]{1,0:T(8,128)S(1)} %copy-done.2), kind=kOutput, calls=%fused_computation.85 | convolution fusion | flops 3221225472 | bytes 6815744 | tf_op jit(solution)/shard_map/dot_general | solution.py:28
  281.9 1.6 collective-permute-start.2
  283.5 12.6 %collective-permute-done.2 = f32[256,512]{1,0:T(8,128)S(1)} collective-permute-done((f32[256,512]{1,0:T(8,128)S(1)}, f32[256,512]{1,0:T(8,128)S(1)}, u32[]{:S(2)}, u32[]{:S(2)}) %collective-permute-start.2) | collective-permute-done | bytes 524320 | tf_op jit(solution)/shard_map/ppermute | solution.py:24
  296.2 1.0 fusion.7
  297.2 1.6 multiply_reduce_fusion.1
  299.8 0.4 fusion.15
  300.5 0.4 select_subtract_fusion.8
  300.9 0.4 fusion.36
  301.7 0.4 select_subtract_fusion.7
  302.8 0.4 select_subtract_fusion.6
  304.0 0.4 select_subtract_fusion.5
  304.8 0.6 convolution_divide_fusion.2
  305.4 1.1 fusion.6
  306.5 3.3 collective-permute-start.3
  309.8 11.8 %collective-permute-done.3 = f32[256,512]{1,0:T(8,128)S(1)} collective-permute-done((f32[256,512]{1,0:T(8,128)S(1)}, f32[256,512]{1,0:T(8,128)S(1)}, u32[]{:S(2)}, u32[]{:S(2)}) %collective-permute-start.3) | collective-permute-done | bytes 524320 | tf_op jit(solution)/shard_map/ppermute | solution.py:24
  321.7 2.0 fusion.5
  323.7 1.6 multiply_reduce_fusion
  326.4 0.4 fusion.16
  327.0 0.4 select_subtract_fusion.3
  328.2 0.4 select_subtract_fusion.2
  329.4 0.4 select_subtract_fusion.1
  329.8 1.1 fusion.47
  331.3 1.5 select_subtract_fusion
  333.2 1.6 convolution_divide_fusion.1
  334.8 1.8 fusion.4
  336.6 1.3 fusion.8
  338.4 4.5 %fusion.49 = f32[2048,64]{0,1:T(8,128)} fusion(f32[2048,256]{1,0:T(8,128)} %copy-done.3, f32[256,64]{0,1:T(8,128)S(1)} %fusion.17), kind=kOutput, calls=%fused_computation.100 | convolution fusion | flops 402653184 | bytes 2686976 | tf_op jit(solution)/shard_map/dot_general | solution.py:28
  (49 shorter events, 8.8 us)
Async XLA Ops:
  7.2 68.6 %copy-start = (bf16[16,4,128,128]{3,2,1,0:T(8,128)(2,1)S(1)}, bf16[16,4,128,128]{3,2,1,0:T(8,128)(2,1)}, u32[]{:S(2)}) copy-start(bf16[16,4,128,128]{3,2,1,0:T(8,128)(2,1)} %param.6) | copy-start | bytes 6291460
  7.2 237.9 %all-gather.2.cloned.1.call-start = ((), (), s32[]{:S(2)}) async-start(), calls=%async_computation | async-start | bytes 37748736 | tf_op jit(solution)/shard_map/all_gather | solution.py:66
  7.2 48.8 %collective-permute-start = (bf16[2048,512]{1,0:T(8,128)(2,1)}, bf16[2048,512]{1,0:T(8,128)(2,1)}, u32[]{:S(2)}, u32[]{:S(2)}) collective-permute-start(bf16[2048,512]{1,0:T(8,128)(2,1)} %param.8), channel_id=1, source_target_pairs={{0,8},{8,16},{16,24},{24,32},{32,40},{40,48},{48,56},{56,64},{64,7... | collective-permute-start | bytes 6291464 | tf_op jit(solution)/shard_map/ppermute | solution.py:15
  12.2 49.3 %collective-permute-start.1 = (bf16[2048,512]{1,0:T(8,128)(2,1)}, bf16[2048,512]{1,0:T(8,128)(2,1)}, u32[]{:S(2)}, u32[]{:S(2)}) collective-permute-start(bf16[2048,512]{1,0:T(8,128)(2,1)} %param.8), channel_id=1, source_target_pairs={{8,0},{16,8},{24,16},{32,24},{40,32},{48,40},{56,48},{64,56},{72,6... | collective-permute-start | bytes 6291464 | tf_op jit(solution)/shard_map/ppermute | solution.py:18
  83.0 177.2 %copy-start.8 = (f32[512,256]{1,0:T(8,128)S(1)}, f32[512,256]{1,0:T(8,128)}, u32[]{:S(2)}) copy-start(f32[512,256]{1,0:T(8,128)} %param.9) | copy-start | bytes 1572868
  275.5 2.3 copy-start.2
  277.9 4.0 %copy-start.3 = (f32[2048,256]{1,0:T(8,128)}, f32[2048,256]{1,0:T(8,128)S(1)}, u32[]{:S(2)}) copy-start(f32[2048,256]{1,0:T(8,128)S(1)} %convolution_divide_fusion) | copy-start | bytes 6291460
  277.9 18.3 %copy-start.7 = (f32[512,256]{1,0:T(8,128)S(1)}, f32[512,256]{1,0:T(8,128)}, u32[]{:S(2)}) copy-start(f32[512,256]{1,0:T(8,128)} %param.10) | copy-start | bytes 1572868
  281.9 14.2 %collective-permute-start.2 = (f32[256,512]{1,0:T(8,128)S(1)}, f32[256,512]{1,0:T(8,128)S(1)}, u32[]{:S(2)}, u32[]{:S(2)}) collective-permute-start(f32[256,512]{1,0:T(8,128)S(1)} %fusion.34), channel_id=1, source_target_pairs={{0,8},{8,0},{16,24},{24,16},{32,40},{40,32},{48,56},{56,48},{64,72... | collective-permute-start | bytes 1572872 | tf_op jit(solution)/shard_map/ppermute | solution.py:24
  305.4 21.0 %copy-start.5 = (f32[512,256]{1,0:T(8,128)}, f32[512,256]{1,0:T(8,128)S(1)}, u32[]{:S(2)}) copy-start(f32[512,256]{1,0:T(8,128)S(1)} %convolution_divide_fusion.2) | copy-start | bytes 1572868
  306.5 15.1 %collective-permute-start.3 = (f32[256,512]{1,0:T(8,128)S(1)}, f32[256,512]{1,0:T(8,128)S(1)}, u32[]{:S(2)}, u32[]{:S(2)}) collective-permute-start(f32[256,512]{1,0:T(8,128)S(1)} %fusion.6), channel_id=1, source_target_pairs={{0,16},{8,24},{16,0},{24,8},{32,48},{40,56},{48,32},{56,40},{64,80... | collective-permute-start | bytes 1572872 | tf_op jit(solution)/shard_map/ppermute | solution.py:24
  323.7 5.7 %copy-start.4 = (f32[512,256]{1,0:T(8,128)}, f32[512,256]{1,0:T(8,128)S(1)}, u32[]{:S(2)}) copy-start(f32[512,256]{1,0:T(8,128)S(1)} %fusion.5) | copy-start | bytes 1572868
  331.3 11.6 %copy-start.1 = (bf16[16,4,128,128]{3,2,1,0:T(8,128)(2,1)S(1)}, bf16[16,4,128,128]{3,2,1,0:T(8,128)(2,1)}, u32[]{:S(2)}) copy-start(bf16[16,4,128,128]{3,2,1,0:T(8,128)(2,1)} %param.6) | copy-start | bytes 6291460
  338.0 4.9 %copy-start.6 = (f32[256,256]{1,0:T(8,128)}, f32[256,256]{1,0:T(8,128)S(1)}, u32[]{:S(2)}) copy-start(f32[256,256]{1,0:T(8,128)S(1)} %fusion.8) | copy-start | bytes 786436
Sparse Core Ops, SparseCore 0:
  83.1 161.8 all-gather.1
